TPU v7x, 128 devices: a whole 4x4x4 slice. The times are simulated.
128 devices in a mesh: tok: 8 (over x, z_hi), feat: 16 (over y, z_lo, core).
Axes of the slice: x: 4, y: 4, z: 4 (z_hi: 2, z_lo: 2; z = z_hi * 2 + z_lo), core: 2. Of those that a mesh axis runs over, the one named last changes fastest.
Arguments:
- resid: bfloat16 [2048, 8192], P(None, ('tok', 'feat')), may hold values from -6 to 6
- resid_grad: bfloat16 [2048, 8192], P(None, ('tok', 'feat')), may hold values from -6 to 6
- active: int32 [16, 20], P('tok'), may hold values from 0 to 79, all different within a row
- w_enc: bfloat16 [8192, 10240], P(None, 'feat'), may hold values from -0.0625 to 0.0625
- b_enc: float32 [10240], P('feat'), may hold values from -3 to 3
- w_dec: bfloat16 [10240, 8192], P('feat'), may hold values from -0.25 to 0.25
- b_dec: float32 [8192], P('feat'), may hold values from -3 to 3
Outputs:
- feature_attr: float32 [2048, 10240], P('tok', 'feat')
- error: float32 [2048, 8192], P('tok', 'feat')
- error_attr: float32 [2048], P('tok')
Inputs may be any that keep to these rules, and one draw needn't show every extreme that they name: `active`: each row lists 20 different feature blocks; every block is listed by some tile.
All inputs are finite; a program needn't handle non-finite values.
Results may differ from a plain program's by a relative error of at most 0.012.
Values may be sent and summed in bfloat16 or wider, within the bound.
A program may use at most 128 MiB of HBM per device.

v0:
```python
import jax
import jax.numpy as jnp
from jax import lax
from jax.sharding import PartitionSpec as P

BLOCK = 128
TILE = 128


def gather_rows(part):
    n_tok = lax.axis_size("tok")
    total, width = part.shape
    own = part.T.reshape(width, n_tok, total // n_tok).transpose(1, 0, 2)
    own = lax.all_to_all(own, "tok", split_axis=0, concat_axis=0, tiled=True)
    cols = lax.all_gather(own, "feat", axis=1, tiled=False)
    return cols.reshape(-1, total // n_tok)


def per_device(resid, resid_grad, active, w_enc, b_enc, w_dec, b_dec):
    rows_x = gather_rows(resid)
    rows_g = gather_rows(resid_grad)
    tok_rows = rows_x.shape[1]
    feat_dev = w_enc.shape[1]
    blocks = feat_dev // BLOCK
    tiles_dev = active.shape[0]
    block_ids = lax.axis_index("feat") * blocks + jnp.arange(blocks, dtype=jnp.int32)
    hits = jnp.any(active[:, :, None] == block_ids[None, None, :], axis=1).astype(jnp.float32)
    pre = (
        lax.dot_general(rows_x, w_enc, (((0,), (0,)), ((), ())), preferred_element_type=jnp.float32)
        + b_enc
    )
    shaped = jnp.maximum(pre, 0.0).reshape(tiles_dev, TILE, blocks, BLOCK) * hits[:, None, :, None]
    acts = shaped.reshape(tok_rows, feat_dev).astype(jnp.bfloat16)
    partial_recon = jnp.dot(acts, w_dec, preferred_element_type=jnp.float32)
    recon_share = lax.psum_scatter(
        partial_recon.astype(jnp.bfloat16), "feat", scatter_dimension=1, tiled=True
    ).astype(jnp.float32)
    share = recon_share.shape[1]
    start = lax.axis_index("feat") * share
    own_x = lax.dynamic_slice_in_dim(rows_x, start, share, 0).T
    own_g = lax.dynamic_slice_in_dim(rows_g, start, share, 0).T
    recon = recon_share + b_dec
    error = own_x.astype(jnp.float32) - recon
    local_terms = jnp.sum(error * own_g.astype(jnp.float32), axis=1)
    error_attr = lax.psum(local_terms, "feat")
    proj = lax.dot_general(
        rows_g, w_dec, (((0,), (1,)), ((), ())), preferred_element_type=jnp.float32
    )
    feature_attr = acts.astype(jnp.float32) * proj
    return (feature_attr, error, error_attr)


def solution(mesh):
    placed = (
        P(None, ("tok", "feat")),
        P(None, ("tok", "feat")),
        P("tok", None),
        P(None, "feat"),
        P("feat"),
        P("feat", None),
        P("feat"),
    )
    return jax.shard_map(
        per_device,
        mesh=mesh,
        in_specs=placed,
        out_specs=(P("tok", "feat"), P("tok", "feat"), P("tok")),
        check_vma=False,
    )
```

profile of v0, /device:TPU:2, one launch (start us, length us, event | category | flops | bytes accessed | tf_op | source)
XLA Modules:
  0.0 207.7 jit_solution(12167993486928577080)
XLA Ops:
  7.2 0.0 copy-start.3
  7.2 0.0 all-gather.5.cloned.1.call-start
  7.2 1.0 copy.35
  8.3 15.0 %all_to_all.10 = bf16[8,64,256]{2,1,0:T(8,128)(2,1)S(1)} all-to-all(bf16[8,64,256]{2,1,0:T(8,128)(2,1)S(1)} %copy.27), channel_id=1, replica_groups=mesh['tok'=8,'feat'=16] {'tok'}, dimensions={0} | all-to-all | bytes 524288 | tf_op jit(solution)/shard_map/all_to_all | solution.py:14
  23.2 0.9 copy.28
  24.1 0.0 all-gather.5.cloned.1.call-update
  24.1 0.0 all-gather.7.cloned.1.call-start
  24.2 1.0 copy.38
  25.2 11.0 %all_to_all.11 = bf16[8,64,256]{2,1,0:T(8,128)(2,1)S(1)} all-to-all(bf16[8,64,256]{2,1,0:T(8,128)(2,1)S(1)} %copy.32), channel_id=1, replica_groups=mesh['tok'=8,'feat'=16] {'tok'}, dimensions={0} | all-to-all | bytes 524288 | tf_op jit(solution)/shard_map/all_to_all | solution.py:14
  36.3 0.9 copy.33
  37.1 0.0 all-gather.7.cloned.1.call-update
  37.1 0.0 reduce-scatter.2.cloned.1.call-start
  37.2 0.0 copy-done.3
  37.2 0.2 compare_reduce_fusion
  37.4 0.1 copy.30
  37.5 0.2 mul.24
  37.8 0.2 copy.31
  38.0 22.3 %all-gather.5.cloned.1.call-done = bf16[8,1024,256]{2,0,1:T(8,128)(2,1)} async-done(((bf16[8,64,256]{2,0,1:T(8,128)(2,1)}), bf16[8,1024,256]{2,0,1:T(8,128)(2,1)}) %all-gather.5.cloned.1.call-update) | async-done | bytes 4194320 | tf_op jit(solution)/shard_map/all_gather | solution.py:15
  60.3 7.4 %copy.29 = bf16[8,1024,256]{1,0,2:T(8,128)(2,1)} copy(bf16[8,1024,256]{2,0,1:T(8,128)(2,1)} %all-gather.5.cloned.1.call-done) | data formatting | bytes 8388608 | tf_op jit(solution)/shard_map/all_gather | solution.py:15
  67.8 0.0 copy-start.4
  67.8 0.0 slice-start
  67.8 6.7 %copy.36 = bf16[32,8,8,1024]{3,1,2,0:T(8,128)(2,1)S(1)} copy(bf16[32,8,8,1024]{3,2,1,0:T(8,128)(2,1)} %bitcast.38) | data formatting | bytes 8388608
  74.5 0.0 copy-start
  74.5 2.0 copy-done
  76.4 0.0 copy-done.4
  76.4 0.0 slice-start.1
  76.4 0.0 slice-start.2
  76.4 6.5 %fusion.2 = bf16[256,640]{1,0:T(8,128)(2,1)S(1)} fusion(f32[256,640]{1,0:T(8,128)S(1)} %copy.31, bf16[8192,256]{0,1:T(8,128)(2,1)S(1)} %bitcast.40, bf16[8192,640]{1,0:T(8,128)(2,1)} %param.10, f32[640]{0:T(1024)S(1)} %copy-done.4), kind=kOutput, calls=%fused_computation.5 | convolution fusion | flops 2685009920 | bytes 15665664 | tf_op jit(solution)/shard_map/dot_general | solution.py:29
  83.0 0.0 slice-done
  83.0 0.0 slice-done.1
  83.0 0.0 slice-done.2
  83.0 5.0 %convolution_convert_fusion = bf16[256,8192]{1,0:T(8,128)(2,1)} fusion(bf16[256,640]{1,0:T(8,128)(2,1)S(1)} %fusion.2, bf16[640,8192]{1,0:T(8,128)(2,1)S(1)} %bitcast.51), kind=kOutput, calls=%fused_computation | convolution fusion | flops 2686451712 | bytes 15007744 | tf_op jit(solution)/shard_map/dot_general | solution.py:34
  88.0 0.0 reduce-scatter.2.cloned.1.call-update
  88.0 11.9 %all-gather.7.cloned.1.call-done = bf16[8,1024,256]{2,0,1:T(8,128)(2,1)} async-done(((bf16[8,64,256]{2,0,1:T(8,128)(2,1)}), bf16[8,1024,256]{2,0,1:T(8,128)(2,1)}) %all-gather.7.cloned.1.call-update) | async-done | bytes 4194320 | tf_op jit(solution)/shard_map/all_gather | solution.py:15
  99.9 7.4 %copy.34 = bf16[8,1024,256]{1,0,2:T(8,128)(2,1)} copy(bf16[8,1024,256]{2,0,1:T(8,128)(2,1)} %all-gather.7.cloned.1.call-done) | data formatting | bytes 8388608 | tf_op jit(solution)/shard_map/all_gather | solution.py:15
  107.3 6.5 %copy.39 = bf16[32,8,8,1024]{3,1,2,0:T(8,128)(2,1)S(1)} copy(bf16[32,8,8,1024]{3,2,1,0:T(8,128)(2,1)} %bitcast.39) | data formatting | bytes 8388608
  113.9 0.0 copy-start.1
  113.9 1.9 copy-done.1
  115.8 0.0 copy-start.2
  115.8 7.2 %convolution_multiply_fusion = f32[256,640]{1,0:T(8,128)} fusion(bf16[8192,256]{0,1:T(8,128)(2,1)S(1)} %bitcast.42, bf16[640,8192]{1,0:T(8,128)(2,1)} %param.12, bf16[256,640]{1,0:T(8,128)(2,1)S(1)} %fusion.2), kind=kOutput, calls=%fused_computation.1 | convolution fusion | flops 2684682240 | bytes 15663104 | tf_op jit(solution)/shard_map/dot_general | solution.py:46
  123.0 47.7 %reduce-scatter.2.cloned.1.call-done = bf16[256,512]{1,0:T(8,128)(2,1)} async-done(((bf16[256,8192]{1,0:T(8,128)(2,1)}), bf16[256,512]{1,0:T(8,128)(2,1)}) %reduce-scatter.2.cloned.1.call-update) | async-done | bytes 262160 | tf_op jit(solution)/shard_map/reduce_scatter | solution.py:35
  170.7 0.0 copy-done.2
  170.7 2.0 fusion.3
  172.7 28.5 %psum.7 = f32[256]{0:T(256)} all-reduce(f32[256]{0:T(256)S(1)} %get-tuple-element.3), channel_id=1, replica_groups=mesh['tok'=8,'feat'=16] {'feat'}, use_global_device_ids=true, to_apply=%region_3.0 | all-reduce | flops 256 | bytes 2048 | tf_op jit(solution)/shard_map/psum | solution.py:45
  (6 shorter events, 0.2 us)
Async XLA Ops:
  7.2 30.0 %copy-start.3 = (s32[2,20]{1,0:T(2,128)S(1)}, s32[2,20]{1,0:T(2,128)}, u32[]{:S(2)}) copy-start(s32[2,20]{1,0:T(2,128)} %param.9) | copy-start | bytes 484
  7.2 53.2 %all-gather.5.cloned.1.call-start = ((), (), s32[]{:S(2)}) async-start(), calls=%async_computation.4 | async-start | bytes 4456448 | tf_op jit(solution)/shard_map/all_gather | solution.py:15
  24.1 75.8 %all-gather.7.cloned.1.call-start = ((), (), s32[]{:S(2)}) async-start(), calls=%async_computation.5 | async-start | bytes 4456448 | tf_op jit(solution)/shard_map/all_gather | solution.py:15
  37.1 133.6 %reduce-scatter.2.cloned.1.call-start = ((), (), s32[]{:S(2)}) async-start(), calls=%async_computation.3 | async-start | bytes 4456448 | tf_op jit(solution)/shard_map/reduce_scatter | solution.py:35
  67.8 8.7 %copy-start.4 = (f32[640]{0:T(1024)S(1)}, f32[640]{0:T(1024)}, u32[]{:S(2)}) copy-start(f32[640]{0:T(1024)} %param.11) | copy-start | bytes 7684
  67.8 15.2 %slice-start = ((s8[10485760]{0:T(1024)(128)(4,1)}), s8[4194304]{0:T(1024)(128)(4,1)S(1)}, s32[]{:S(2)}) async-start(s8[10485760]{0:T(1024)(128)(4,1)} %bitcast.50), calls=%async_computation.6 | async-start | bytes 8388608
  74.5 2.0 copy-start
  76.4 6.6 %slice-start.1 = ((s8[10485760]{0:T(1024)(128)(4,1)}), s8[4194304]{0:T(1024)(128)(4,1)S(1)}, s32[]{:S(2)}) async-start(s8[10485760]{0:T(1024)(128)(4,1)} %bitcast.50), calls=%async_computation.7 | async-start | bytes 8388608
  76.4 6.6 %slice-start.2 = ((s8[10485760]{0:T(1024)(128)(4,1)}), s8[2097152]{0:T(1024)(128)(4,1)S(1)}, s32[]{:S(2)}) async-start(s8[10485760]{0:T(1024)(128)(4,1)} %bitcast.50), calls=%async_computation.8 | async-start | bytes 4194304
  113.9 1.9 copy-start.1
  115.8 54.9 %copy-start.2 = (f32[512]{0:T(512)S(1)}, f32[512]{0:T(512)}, u32[]{:S(2)}) copy-start(f32[512]{0:T(512)} %param.13) | copy-start | bytes 6148
Sparse Core Ops, SparseCore 0:
  24.2 36.0 all-gather.4
  62.6 37.2 all-gather.6
  102.3 68.3 reduce-scatter.1
where the time goes:
time: 208 us
  waiting for transfers between devices  82 us (39%)
  blocking collectives  54.5 us (26%)
  local copies, waits for them, and re-layouts  36.4 us (18%)
  matrix products  18.7 us (9%)
  between operations  13.9 us (7%)
  other arithmetic  2.22 us (1%)
    reduce_scatter x1, waiting for transfers between devices, per_device(): lax.psum_scatter(partial_recon.astype(jnp.bfloat16), 'feat', scatter_dime...  47.7 us
    all_gather x2, waiting for transfers between devices, gather_rows(): cols = lax.all_gather(own, 'feat', axis=1, tiled=False)  34.2 us
    psum x1, blocking collectives, per_device(): error_attr = lax.psum(local_terms, 'feat')  28.5 us
    all_to_all x2, blocking collectives, gather_rows(): own = lax.all_to_all(own, 'tok', split_axis=0, concat_axis=0, tiled=True)  26 us
    unnamed x21, local copies, waits for them, and re-layouts  19.2 us
    all_gather x2, local copies, waits for them, and re-layouts, gather_rows(): cols = lax.all_gather(own, 'feat', axis=1, tiled=False)  14.8 us
    dot_general x1, matrix products, per_device(): lax.dot_general(rows_g, w_dec, (((0,), (1,)), ((), ())), preferred_elemen...  7.16 us
    dot_general x1, matrix products, per_device(): lax.dot_general(rows_x, w_enc, (((0,), (0,)), ((), ())), preferred_elemen...  6.53 us
  transfers between devices with their start and end apart: 3, of which 3 were waited for; matrix products, arithmetic and copies ran while one was open for 24% of the time, Pallas kernels for 0%

commit v1 on v0

--- a/solution.py
+++ b/solution.py
@@ -42,7 +42,7 @@
     recon = recon_share + b_dec
     error = own_x.astype(jnp.float32) - recon
     local_terms = jnp.sum(error * own_g.astype(jnp.float32), axis=1)
-    error_attr = lax.psum(local_terms, "feat")
+    error_attr = jnp.sum(lax.all_gather(local_terms, "feat"), axis=0)
     proj = lax.dot_general(
         rows_g, w_dec, (((0,), (1,)), ((), ())), preferred_element_type=jnp.float32
     )

time: 208 us -> 198 us (0.952)
  blocking collectives: 54.5 us -> 42 us
    psum x1 -> x0, blocking collectives: 28.5 us -> none  [per_device(): error_attr = lax.psum(local_terms, 'feat')]
    all_gather x0 -> x1, blocking collectives: none -> 16 us  [per_device(): error_attr = jnp.sum(lax.all_gather(local_terms, 'feat'), axis=0)]
  transfers between devices with their start and end apart: 3 -> 3, of which waited for: 3 -> 3; matrix products, arithmetic and copies ran while one was open for 24% -> 25% of each run, Pallas kernels for 0% -> 0%
where the time goes in v1:
time: 198 us; the launch traced here: 196 us
  waiting for transfers between devices  81.9 us (41%)
  blocking collectives  42 us (21%)
  local copies, waits for them, and re-layouts  36.4 us (18%)
  matrix products  18.8 us (9%)
  between operations  13.9 us (7%)
  other arithmetic  2.81 us (1%)
    reduce_scatter x1, waiting for transfers between devices, per_device(): lax.psum_scatter(partial_recon.astype(jnp.bfloat16), 'feat', scatter_dime...  47.7 us
    all_gather x2, waiting for transfers between devices, gather_rows(): cols = lax.all_gather(own, 'feat', axis=1, tiled=False)  34.1 us
    all_to_all x2, blocking collectives, gather_rows(): own = lax.all_to_all(own, 'tok', split_axis=0, concat_axis=0, tiled=True)  26 us
    unnamed x21, local copies, waits for them, and re-layouts  19.2 us
    all_gather x1, blocking collectives, per_device(): error_attr = jnp.sum(lax.all_gather(local_terms, 'feat'), axis=0)  16 us
    all_gather x2, local copies, waits for them, and re-layouts, gather_rows(): cols = lax.all_gather(own, 'feat', axis=1, tiled=False)  14.8 us
    dot_general x1, matrix products, per_device(): lax.dot_general(rows_g, w_dec, (((0,), (1,)), ((), ())), preferred_elemen...  7.17 us
    dot_general x1, matrix products, per_device(): lax.dot_general(rows_x, w_enc, (((0,), (0,)), ((), ())), preferred_elemen...  6.53 us
  transfers between devices with their start and end apart: 3, of which 3 were waited for; matrix products, arithmetic and copies ran while one was open for 25% of the time, Pallas kernels for 0%

profile of v1, /device:TPU:2, one launch (start us, length us, event | category | flops | bytes accessed | tf_op | source)
XLA Modules:
  0.0 195.8 jit_solution(19209309117726439)
XLA Ops:
  7.2 0.0 copy-start.3
  7.2 0.0 all-gather.7.cloned.1.call-start
  7.2 1.0 copy.35
  8.3 15.0 %all_to_all.10 = bf16[8,64,256]{2,1,0:T(8,128)(2,1)S(1)} all-to-all(bf16[8,64,256]{2,1,0:T(8,128)(2,1)S(1)} %copy.27), channel_id=1, replica_groups=mesh['tok'=8,'feat'=16] {'tok'}, dimensions={0} | all-to-all | bytes 524288 | tf_op jit(solution)/shard_map/all_to_all | solution.py:14
  23.2 0.9 copy.28
  24.1 0.0 all-gather.7.cloned.1.call-update
  24.1 0.0 all-gather.9.cloned.1.call-start
  24.2 1.0 copy.38
  25.2 11.0 %all_to_all.11 = bf16[8,64,256]{2,1,0:T(8,128)(2,1)S(1)} all-to-all(bf16[8,64,256]{2,1,0:T(8,128)(2,1)S(1)} %copy.32), channel_id=1, replica_groups=mesh['tok'=8,'feat'=16] {'tok'}, dimensions={0} | all-to-all | bytes 524288 | tf_op jit(solution)/shard_map/all_to_all | solution.py:14
  36.3 0.9 copy.33
  37.1 0.0 all-gather.9.cloned.1.call-update
  37.1 0.0 reduce-scatter.2.cloned.1.call-start
  37.2 0.0 copy-done.3
  37.2 0.2 compare_reduce_fusion
  37.4 0.1 copy.30
  37.5 0.2 mul.24
  37.8 0.2 copy.31
  38.0 22.3 %all-gather.7.cloned.1.call-done = bf16[8,1024,256]{2,0,1:T(8,128)(2,1)} async-done(((bf16[8,64,256]{2,0,1:T(8,128)(2,1)}), bf16[8,1024,256]{2,0,1:T(8,128)(2,1)}) %all-gather.7.cloned.1.call-update) | async-done | bytes 4194320 | tf_op jit(solution)/shard_map/all_gather | solution.py:15
  60.3 7.4 %copy.29 = bf16[8,1024,256]{1,0,2:T(8,128)(2,1)} copy(bf16[8,1024,256]{2,0,1:T(8,128)(2,1)} %all-gather.7.cloned.1.call-done) | data formatting | bytes 8388608 | tf_op jit(solution)/shard_map/all_gather | solution.py:15
  67.8 0.0 copy-start.4
  67.8 0.0 slice-start
  67.8 6.7 %copy.36 = bf16[32,8,8,1024]{3,1,2,0:T(8,128)(2,1)S(1)} copy(bf16[32,8,8,1024]{3,2,1,0:T(8,128)(2,1)} %bitcast.39) | data formatting | bytes 8388608
  74.5 0.0 copy-start
  74.5 2.0 %copy-done = bf16[32,8,8,1024]{3,1,2,0:T(8,128)(2,1)} copy-done((bf16[32,8,8,1024]{3,1,2,0:T(8,128)(2,1)}, bf16[32,8,8,1024]{3,1,2,0:T(8,128)(2,1)S(1)}, u32[]{:S(2)}) %copy-start) | copy-done | bytes 4194328
  76.4 0.0 copy-done.4
  76.4 0.0 slice-start.1
  76.4 0.0 slice-start.2
  76.4 6.5 %fusion.2 = bf16[256,640]{1,0:T(8,128)(2,1)S(1)} fusion(f32[256,640]{1,0:T(8,128)S(1)} %copy.31, bf16[8192,256]{0,1:T(8,128)(2,1)S(1)} %bitcast.41, bf16[8192,640]{1,0:T(8,128)(2,1)} %param.10, f32[640]{0:T(1024)S(1)} %copy-done.4), kind=kOutput, calls=%fused_computation.5 | convolution fusion | flops 2685009920 | bytes 15665664 | tf_op jit(solution)/shard_map/dot_general | solution.py:29
  83.0 0.0 slice-done
  83.0 0.0 slice-done.1
  83.0 0.0 slice-done.2
  83.0 5.1 %convolution_convert_fusion = bf16[256,8192]{1,0:T(8,128)(2,1)} fusion(bf16[256,640]{1,0:T(8,128)(2,1)S(1)} %fusion.2, bf16[640,8192]{1,0:T(8,128)(2,1)S(1)} %bitcast.53), kind=kOutput, calls=%fused_computation | convolution fusion | flops 2686451712 | bytes 15007744 | tf_op jit(solution)/shard_map/dot_general | solution.py:34
  88.1 0.0 reduce-scatter.2.cloned.1.call-update
  88.1 11.8 %all-gather.9.cloned.1.call-done = bf16[8,1024,256]{2,0,1:T(8,128)(2,1)} async-done(((bf16[8,64,256]{2,0,1:T(8,128)(2,1)}), bf16[8,1024,256]{2,0,1:T(8,128)(2,1)}) %all-gather.9.cloned.1.call-update) | async-done | bytes 4194320 | tf_op jit(solution)/shard_map/all_gather | solution.py:15
  99.9 7.4 %copy.34 = bf16[8,1024,256]{1,0,2:T(8,128)(2,1)} copy(bf16[8,1024,256]{2,0,1:T(8,128)(2,1)} %all-gather.9.cloned.1.call-done) | data formatting | bytes 8388608 | tf_op jit(solution)/shard_map/all_gather | solution.py:15
  107.3 6.5 %copy.39 = bf16[32,8,8,1024]{3,1,2,0:T(8,128)(2,1)S(1)} copy(bf16[32,8,8,1024]{3,2,1,0:T(8,128)(2,1)} %bitcast.40) | data formatting | bytes 8388608
  113.9 0.0 copy-start.1
  113.9 1.9 copy-done.1
  115.8 0.0 copy-start.2
  115.8 7.2 %convolution_multiply_fusion = f32[256,640]{1,0:T(8,128)} fusion(bf16[8192,256]{0,1:T(8,128)(2,1)S(1)} %bitcast.43, bf16[640,8192]{1,0:T(8,128)(2,1)} %param.12, bf16[256,640]{1,0:T(8,128)(2,1)S(1)} %fusion.2), kind=kOutput, calls=%fused_computation.1 | convolution fusion | flops 2684682240 | bytes 15663104 | tf_op jit(solution)/shard_map/dot_general | solution.py:46
  123.0 47.7 %reduce-scatter.2.cloned.1.call-done = bf16[256,512]{1,0:T(8,128)(2,1)} async-done(((bf16[256,8192]{1,0:T(8,128)(2,1)}), bf16[256,512]{1,0:T(8,128)(2,1)}) %reduce-scatter.2.cloned.1.call-update) | async-done | bytes 262160 | tf_op jit(solution)/shard_map/reduce_scatter | solution.py:35
  170.7 0.0 copy-done.2
  170.7 2.0 %fusion.3 = (f32[256]{0:T(256)S(1)}, f32[256,512]{1,0:T(8,128)}) fusion(bf16[8192,256]{0,1:T(8,128)(2,1)} %bitcast.44, s32[]{:T(128)S(6)} %select_n.4, f32[512]{0:T(512)S(1)} %copy-done.2, bf16[256,512]{1,0:T(8,128)(2,1)} %reduce-scatter.2.cloned.1.call-done, bf16[8192,256]{0,1:T(8,128)(2,1)} %bitcast.42), kind=kLoop, calls=%fused_computation.8 | loop fusion | flops 917248 | bytes 1313796 | tf_op jit(solution)/shard_map/reduce_sum | solution.py:44
  172.7 16.0 %all-gather.3 = f32[16,1,256]{2,1,0:T(1,128)S(1)} all-gather(f32[1,1,256]{2,1,0:T(1,128)S(1)} %bitcast.51), channel_id=4, replica_groups=mesh['tok'=8,'feat'=16] {'feat'}, dimensions={0}, use_global_device_ids=true | all-gather | bytes 17408 | tf_op jit(solution)/shard_map/all_gather | solution.py:45
  188.7 0.6 reduce_sum.19
  (6 shorter events, 0.2 us)
Async XLA Ops:
  7.2 30.0 %copy-start.3 = (s32[2,20]{1,0:T(2,128)S(1)}, s32[2,20]{1,0:T(2,128)}, u32[]{:S(2)}) copy-start(s32[2,20]{1,0:T(2,128)} %param.9) | copy-start | bytes 484
  7.2 53.2 %all-gather.7.cloned.1.call-start = ((), (), s32[]{:S(2)}) async-start(), calls=%async_computation.4 | async-start | bytes 4456448 | tf_op jit(solution)/shard_map/all_gather | solution.py:15
  24.1 75.8 %all-gather.9.cloned.1.call-start = ((), (), s32[]{:S(2)}) async-start(), calls=%async_computation.5 | async-start | bytes 4456448 | tf_op jit(solution)/shard_map/all_gather | solution.py:15
  37.1 133.5 %reduce-scatter.2.cloned.1.call-start = ((), (), s32[]{:S(2)}) async-start(), calls=%async_computation.3 | async-start | bytes 4456448 | tf_op jit(solution)/shard_map/reduce_scatter | solution.py:35
  67.8 8.7 %copy-start.4 = (f32[640]{0:T(1024)S(1)}, f32[640]{0:T(1024)}, u32[]{:S(2)}) copy-start(f32[640]{0:T(1024)} %param.11) | copy-start | bytes 7684
  67.8 15.2 %slice-start = ((s8[10485760]{0:T(1024)(128)(4,1)}), s8[4194304]{0:T(1024)(128)(4,1)S(1)}, s32[]{:S(2)}) async-start(s8[10485760]{0:T(1024)(128)(4,1)} %bitcast.52), calls=%async_computation.6 | async-start | bytes 8388608
  74.5 2.0 %copy-start = (bf16[32,8,8,1024]{3,1,2,0:T(8,128)(2,1)}, bf16[32,8,8,1024]{3,1,2,0:T(8,128)(2,1)S(1)}, u32[]{:S(2)}) copy-start(bf16[32,8,8,1024]{3,1,2,0:T(8,128)(2,1)S(1)} %copy.36) | copy-start | bytes 12582916
  76.4 6.6 %slice-start.1 = ((s8[10485760]{0:T(1024)(128)(4,1)}), s8[4194304]{0:T(1024)(128)(4,1)S(1)}, s32[]{:S(2)}) async-start(s8[10485760]{0:T(1024)(128)(4,1)} %bitcast.52), calls=%async_computation.7 | async-start | bytes 8388608
  76.4 6.6 %slice-start.2 = ((s8[10485760]{0:T(1024)(128)(4,1)}), s8[2097152]{0:T(1024)(128)(4,1)S(1)}, s32[]{:S(2)}) async-start(s8[10485760]{0:T(1024)(128)(4,1)} %bitcast.52), calls=%async_computation.8 | async-start | bytes 4194304
  113.9 1.9 copy-start.1
  115.8 54.9 %copy-start.2 = (f32[512]{0:T(512)S(1)}, f32[512]{0:T(512)}, u32[]{:S(2)}) copy-start(f32[512]{0:T(512)} %param.13) | copy-start | bytes 6148
Sparse Core Ops, SparseCore 0:
  24.2 36.0 all-gather.6
  62.6 37.2 all-gather.8
  102.4 68.2 reduce-scatter.1
